TPU v7x, 768 devices: a whole 4x8x12 slice. The times are simulated.
768 devices in a mesh: state: 4 (over x), row: 16 (over y, core), col: 12 (over z).
Axes of the slice: x: 4, y: 8, z: 12, core: 2. Of those that a mesh axis runs over, the one named last changes fastest.
Arguments:
- coeff_rows: bfloat16 [8192, 4096], P('row', 'state'), may hold values from -0.09375 to 0.09375
- coeff_cols: bfloat16 [12288, 4096], P('col', 'state'), may hold values from -0.09375 to 0.09375
- occupation: float32 [4096], P('state'), may hold values from 0.05 to 2
- send_list: int32 [4, 16, 12, 16, 2], P('state', 'row', 'col'), may hold values from 0 to 8
- row_phi: bfloat16 [4, 16, 12, 32, 128, 256], P('state', 'row', 'col'), may hold values from -6 to 6
- col_phi: bfloat16 [4, 16, 12, 32, 128, 256], P('state', 'row', 'col'), may hold values from -6 to 6
Outputs:
- density: float32 [4, 16, 12, 256], P('state', 'row', 'col')
Inputs may be any that keep to these rules, and one draw needn't show every extreme that they name: `send_list`: a value of 8 relays nothing.
All inputs are finite; a program needn't handle non-finite values.
Results may differ from a plain program's by a relative error of at most 0.004.
Values may be sent and summed in bfloat16 or wider, within the bound.
A program may use at most 32 MiB of HBM per device.

v0:
```python
import jax
import jax.numpy as jnp
from jax import lax
from jax.sharding import PartitionSpec as P


def local(coeff_rows, coeff_cols, occupation, send_list, row_phi, col_phi):
    weighted = (coeff_rows.astype(jnp.float32) * occupation[None, :]).astype(jnp.bfloat16)
    partial_block = lax.dot_general(
        weighted, coeff_cols, (((1,), (1,)), ((), ())), preferred_element_type=jnp.float32
    )
    side = coeff_rows.shape[0] // lax.axis_size("state")
    summed = lax.psum(partial_block, "state")
    mine = lax.dynamic_slice_in_dim(summed, lax.axis_index("state") * side, side, 0)
    mine = mine.astype(jnp.bfloat16)
    count = mine.shape[1] // side
    tiles = mine.reshape(side, count, side).transpose(1, 0, 2)
    tiles = jnp.concatenate([tiles, jnp.zeros((1, side, side), jnp.bfloat16)], axis=0)
    picks = send_list[0, 0, 0]
    onehot = (picks[:, :, None] == jnp.arange(count + 1, dtype=jnp.int32)[None, None, :]).astype(
        jnp.bfloat16
    )
    outgoing = jnp.einsum(
        "jkt,tab->jkab", onehot, tiles, preferred_element_type=jnp.float32
    ).astype(jnp.bfloat16)
    received = lax.all_to_all(outgoing, "row", split_axis=0, concat_axis=0, tiled=True)
    received = received.reshape(-1, side, side)
    half = jnp.einsum(
        "tab,tbp->tap", received, col_phi[0, 0, 0], preferred_element_type=jnp.float32
    )
    density = jnp.sum(row_phi[0, 0, 0].astype(jnp.float32) * half, axis=(0, 1))
    return density.reshape(1, 1, 1, -1)


def solution(mesh):
    in_specs = (
        P("row", "state"),
        P("col", "state"),
        P("state"),
        P("state", "row", "col", None, None),
        P("state", "row", "col", None, None, None),
        P("state", "row", "col", None, None, None),
    )
    out_specs = P("state", "row", "col", None)
    return jax.shard_map(local, mesh=mesh, in_specs=in_specs, out_specs=out_specs, check_vma=False)
```

profile of v0, /device:TPU:1, one launch (start us, length us, event | category | flops | bytes accessed | tf_op | source)
XLA Modules:
  0.0 88.6 jit_solution(10074019005860614269)
XLA Ops:
  0.0 0.0 copy-start
  0.0 1.6 %copy-done = bf16[1024,1024]{1,0:T(8,128)(2,1)S(1)} copy-done((bf16[1024,1024]{1,0:T(8,128)(2,1)S(1)}, bf16[1024,1024]{1,0:T(8,128)(2,1)}, u32[]{:S(2)}) %copy-start) | copy-done | bytes 2097176
  1.6 3.9 %fusion.2 = f32[512,1024]{1,0:T(8,128)} fusion(bf16[1024,1024]{1,0:T(8,128)(2,1)S(1)} %copy-done, bf16[512,1024]{1,0:T(8,128)(2,1)} %param.6, f32[1024]{0:T(1024)} %param.8), kind=kOutput, calls=%fused_computation.5 | convolution fusion | flops 1075314688 | bytes 5246976 | tf_op jit(solution)/shard_map/dot_general | solution.py:9
  5.5 0.0 copy-start.3
  5.5 37.7 %all-reduce.2 = bf16[512,1024]{1,0:T(8,128)(2,1)S(1)} all-reduce(f32[512,1024]{1,0:T(8,128)} %fusion.2), channel_id=1, replica_groups=mesh['state'=4,'row'=16,'col'=12] {'state'}, use_global_device_ids=true, to_apply=%region_0.0 | all-reduce | flops 524288 | bytes 3145728 | tf_op jit(solution)/shard_map/psum | solution.py:13
  43.3 0.0 copy-done.3
  43.3 0.5 convolution_convert_fusion
  43.8 0.0 copy-start.1
  43.8 0.0 copy-start.2
  43.8 0.3 copy.8
  44.1 43.2 %all_to_all.5 = bf16[16,2,128,128]{3,2,1,0:T(8,128)(2,1)S(1)} all-to-all(bf16[16,2,128,128]{3,2,1,0:T(8,128)(2,1)S(1)} %copy.8), channel_id=1, replica_groups=mesh['state'=4,'row'=16,'col'=12] {'row'}, dimensions={0} | all-to-all | bytes 2097152 | tf_op jit(solution)/shard_map/all_to_all | solution.py:26
  87.3 0.0 copy-done.1
  87.3 0.0 copy-done.2
  87.3 1.3 %fusion = f32[256]{0:T(256)} fusion(bf16[32,128,128]{2,1,0:T(8,128)(2,1)S(1)} %bitcast.24, bf16[1,1,1,32,128,256]{5,4,3,2,1,0:T(8,128)(2,1)S(1)} %copy-done.1, bf16[1,1,1,32,128,256]{5,4,3,2,1,0:T(8,128)(2,1)S(1)} %copy-done.2), kind=kOutput, calls=%fused_computation.1 | convolution fusion | flops 271580928 | bytes 5243904 | tf_op jit(solution)/shard_map/tab,tbp->tap/dot_general | solution.py:28
  (2 shorter events, 0.1 us)
Async XLA Ops:
  0.0 1.6 %copy-start = (bf16[1024,1024]{1,0:T(8,128)(2,1)S(1)}, bf16[1024,1024]{1,0:T(8,128)(2,1)}, u32[]{:S(2)}) copy-start(bf16[1024,1024]{1,0:T(8,128)(2,1)} %param.7) | copy-start | bytes 6291460
  5.5 37.8 %copy-start.3 = (s32[1,1,1,16,2]{3,4,2,1,0:T(2,128)S(1)}, s32[1,1,1,16,2]{3,4,2,1,0:T(2,128)}, u32[]{:S(2)}) copy-start(s32[1,1,1,16,2]{3,4,2,1,0:T(2,128)} %param.9) | copy-start | bytes 388
  43.8 43.5 %copy-start.1 = (bf16[1,1,1,32,128,256]{5,4,3,2,1,0:T(8,128)(2,1)S(1)}, bf16[1,1,1,32,128,256]{5,4,3,2,1,0:T(8,128)(2,1)}, u32[]{:S(2)}) copy-start(bf16[1,1,1,32,128,256]{5,4,3,2,1,0:T(8,128)(2,1)} %param.10) | copy-start | bytes 6291460
  43.8 43.5 %copy-start.2 = (bf16[1,1,1,32,128,256]{5,4,3,2,1,0:T(8,128)(2,1)S(1)}, bf16[1,1,1,32,128,256]{5,4,3,2,1,0:T(8,128)(2,1)}, u32[]{:S(2)}) copy-start(bf16[1,1,1,32,128,256]{5,4,3,2,1,0:T(8,128)(2,1)} %param.11) | copy-start | bytes 6291460
where the time goes:
time: 88.8 us; the launch traced here: 88.6 us
  blocking collectives  80.9 us (91%)
  matrix products  5.63 us (6%)
  local copies, waits for them, and re-layouts  1.95 us (2%)
    all_to_all x1, blocking collectives, local(): lax.all_to_all(outgoing, 'row', split_axis=0, concat_axis=0, tiled=True)  43.2 us
    psum x1, blocking collectives, local(): summed = lax.psum(partial_block, 'state')  37.7 us
    dot_general x1, matrix products, local(): lax.dot_general(weighted, coeff_cols, (((1,), (1,)), ((), ())), preferred...  3.87 us

commit v1 on v0

v1 whole, which is shorter than its diff:
```python
import functools

import jax
import jax.numpy as jnp
from jax import lax
from jax.experimental import pallas as pl
from jax.experimental.pallas import tpu as pltpu
from jax.sharding import PartitionSpec as P

MESH = pl.DeviceIdType.MESH
CHUNKS = 4
HEAD = 16
OWN, UP, DOWN, FAR = 0, (0, 1, 2, 3), (0, 4, 5, 6), 7


def kernel(
    side, count, occ_ref, list_ref, rows_hbm, cols_hbm, rphi_hbm, cphi_hbm, out_ref,
    rows_v, cols_v, rphi_v, cphi_v, weighted_v, own_v, next_v,
    stage_s, stage_r, plain_s, plain_r, comb_s, comb_r, *rest,
):
    blocks = [[rest[2 * j], rest[2 * j + 1]] for j in range(8)]
    load_sem, xs, xr, ys, yr, ss, sr = rest[16:]
    n_state, n_row = lax.axis_size("state"), lax.axis_size("row")
    chips = n_row // 2
    s, r = lax.axis_index("state"), lax.axis_index("row")
    y, k = r // 2, r % 2
    x_next, x_prev = lax.rem(s + 1, n_state), lax.rem(s + n_state - 1, n_state)
    up = lax.rem(y + 1, chips) * 2 + k
    down = lax.rem(y + chips - 1, chips) * 2 + k
    sibling = y * 2 + 1 - k
    width = count * side // CHUNKS

    barrier = pltpu.get_barrier_semaphore()
    neighbours = ({"state": x_next}, {"state": x_prev}, {"row": up}, {"row": down}, {"row": sibling})
    for who in neighbours:
        pl.semaphore_signal(barrier, inc=1, device_id=who, device_id_type=MESH)

    loads = [
        pltpu.make_async_copy(rows_hbm, rows_v, load_sem.at[0]),
        *(
            pltpu.make_async_copy(
                cols_hbm.at[pl.ds(q * width, width)], cols_v.at[pl.ds(q * width, width)], load_sem.at[1 + q]
            )
            for q in range(CHUNKS)
        ),
        pltpu.make_async_copy(rphi_hbm, rphi_v, load_sem.at[1 + CHUNKS]),
        pltpu.make_async_copy(cphi_hbm, cphi_v, load_sem.at[2 + CHUNKS]),
    ]
    for load in loads:
        load.start()

    picks = list_ref[0, 0, 0].astype(jnp.float32)
    lane = lax.broadcasted_iota(jnp.int32, (n_row, 128), 1)
    picks = jnp.where(
        lane == 0,
        jnp.broadcast_to(picks[:, 0:1], (n_row, 128)),
        jnp.broadcast_to(picks[:, 1:2], (n_row, 128)),
    )
    blocks[OWN][0][pl.ds(0, HEAD), :] = picks.astype(jnp.bfloat16)

    loads[0].wait()
    for j in range(n_state):
        target = lax.rem(s + j, n_state)
        part = rows_v[pl.ds(pl.multiple_of(target * side, side), side), :].astype(jnp.float32)
        weighted_v[pl.ds(j * side, side), :] = (part * occ_ref[...]).astype(jnp.bfloat16)

    sent = []

    def send(src, dst, send_sem, recv_sem, who):
        copy = pltpu.make_async_remote_copy(
            src_ref=src, dst_ref=dst, send_sem=send_sem, recv_sem=recv_sem, device_id=who, device_id_type=MESH
        )
        copy.start()
        sent.append(copy)

    def arrived(dst, send_sem, recv_sem):
        pltpu.make_async_remote_copy(
            src_ref=dst, dst_ref=dst, send_sem=send_sem, recv_sem=recv_sem,
            device_id={"row": sibling}, device_id_type=MESH,
        ).wait_recv()

    def ways(q):
        return (x_next, x_prev) if q % 2 == 0 else (x_prev, x_next)

    def partials(q):
        loads[1 + q].wait()
        product = lax.dot_general(
            weighted_v[...], cols_v[pl.ds(q * width, width), :], (((1,), (1,)), ((), ())),
            preferred_element_type=jnp.float32,
        )
        own_v[q] = product[:side]
        after, before = product[side : 2 * side], product[3 * side :]
        relayed, plain = (after, before) if q % 2 == 0 else (before, after)
        next_v[q] = relayed
        stage_s[q] = product[2 * side : 3 * side].astype(jnp.bfloat16)
        plain_s[q] = plain.astype(jnp.bfloat16)

    def first_sends(q):
        ahead, back = ways(q)
        send(stage_s.at[q], stage_r.at[q], xs.at[0, q], xr.at[0, q], {"state": ahead})
        send(plain_s.at[q], plain_r.at[q], xs.at[1, q], xr.at[1, q], {"state": back})

    def relay(q):
        ahead, _ = ways(q)
        arrived(stage_r.at[q], xs.at[0, q], xr.at[0, q])
        comb_s[q] = (next_v[q] + stage_r[q].astype(jnp.float32)).astype(jnp.bfloat16)
        send(comb_s.at[q], comb_r.at[q], xs.at[2, q], xr.at[2, q], {"state": ahead})

    def span(q):
        return pl.ds(0, HEAD + width) if q == 0 else pl.ds(HEAD + q * width, width)

    def share(j, q):
        send(blocks[j][0].at[span(q)], blocks[j][1].at[span(q)], ss.at[j, q], sr.at[j, q], {"row": sibling})

    def hop(way, h, q):
        path, who = ((UP, up), (DOWN, down))[way]
        if h == 4 and q % 2 != way:
            return
        src = blocks[path[h - 1]][0].at[span(q)]
        dst = blocks[FAR if h == 4 else path[h]][0].at[span(q)]
        send(src, dst, ys.at[way, h - 1, q], yr.at[way, h - 1, q], {"row": who})

    def finish(q):
        arrived(plain_r.at[q], xs.at[1, q], xr.at[1, q])
        arrived(comb_r.at[q], xs.at[2, q], xr.at[2, q])
        total = own_v[q] + plain_r[q].astype(jnp.float32) + comb_r[q].astype(jnp.float32)
        total = total.astype(jnp.bfloat16)
        for t in range(width // side):
            blocks[OWN][0][pl.ds(HEAD + q * width + t * side, side), :] = total[:, t * side : (t + 1) * side]
        hop(0, 1, q)
        hop(1, 1, q)
        share(OWN, q)

    def forward(h, q):
        for way in (0, 1):
            if h == 4 and q % 2 != way:
                continue
            j = FAR if h == 4 else (UP, DOWN)[way][h]
            arrived(blocks[j][0].at[span(q)], ys.at[way, h - 1, q], yr.at[way, h - 1, q])
            if h < 4:
                hop(way, h + 1, q)
            share(j, q)

    row_of = lax.broadcasted_iota(jnp.int32, (HEAD, 128), 0)
    lane_of = lax.broadcasted_iota(jnp.int32, (1, 128), 1)

    def chip_of(j):
        if j == FAR:
            return lax.rem(y + 4, chips)
        if j in UP:
            return lax.rem(y + chips - UP.index(j), chips)
        return lax.rem(y + DOWN.index(j), chips)

    def contract(j, other, total):
        ref = blocks[j][other]
        source = chip_of(j) * 2 + (1 - k if other else k)
        if other:
            for q in range(CHUNKS):
                arrived(ref.at[span(q)], ss.at[j, q], sr.at[j, q])
        mine = jnp.sum(jnp.where(row_of == r, ref[pl.ds(0, HEAD), :].astype(jnp.float32), 0.0), axis=0, keepdims=True)
        got = [None, None]
        wants = [jnp.sum(jnp.where(lane_of == slot, mine, 0.0), axis=1, keepdims=True) for slot in (0, 1)]
        for t in range(count):
            tile = ref[pl.ds(HEAD + t * side, side), :]
            for slot in (0, 1):
                gate = jnp.where(wants[slot] == float(t), 1.0, 0.0)
                gate = jnp.broadcast_to(gate, (side, side)).astype(jnp.bfloat16)
                term = gate * tile
                got[slot] = term if got[slot] is None else got[slot] + term
        for slot in (0, 1):
            m = source * 2 + slot
            half = jnp.dot(got[slot], cphi_v[0, 0, 0, m], preferred_element_type=jnp.float32)
            weighed = rphi_v[0, 0, 0, m].astype(jnp.float32) * half
            total = total + jnp.sum(weighed.reshape(side // 8, 8, weighed.shape[1]), axis=0)
        return total

    partials(0)
    pl.semaphore_wait(barrier, len(neighbours))
    first_sends(0)
    for q in range(1, CHUNKS):
        partials(q)
        first_sends(q)
    relay(0)
    relay(1)
    finish(0)
    relay(2)
    finish(1)
    forward(1, 0)
    relay(3)
    finish(2)
    forward(1, 1)
    finish(3)
    forward(1, 2)
    forward(1, 3)
    for load in loads[1 + CHUNKS :]:
        load.wait()
    for q in range(CHUNKS):
        forward(2, q)
    total = jnp.zeros((8, out_ref.shape[-1]), jnp.float32)
    for j in (OWN, UP[1], DOWN[1]):
        for other in (0, 1):
            total = contract(j, other, total)
    for q in range(CHUNKS):
        forward(3, q)
    for j in (UP[2], DOWN[2]):
        for other in (0, 1):
            total = contract(j, other, total)
    forward(4, 0)
    forward(4, 1)
    for j in (UP[3], DOWN[3]):
        for other in (0, 1):
            total = contract(j, other, total)
    forward(4, 2)
    forward(4, 3)
    for other in (0, 1):
        total = contract(FAR, other, total)
    out_ref[...] = jnp.sum(total, axis=0, keepdims=True)
    for copy in sent:
        copy.wait_send()


def local(coeff_rows, coeff_cols, occupation, send_list, row_phi, col_phi):
    n_state = lax.axis_size("state")
    rows, depth = coeff_rows.shape
    side = rows // n_state
    count = coeff_cols.shape[0] // side
    width = coeff_cols.shape[0] // CHUNKS
    points = row_phi.shape[-1]
    bf16, f32 = jnp.bfloat16, jnp.float32
    dma = pltpu.SemaphoreType.DMA
    vmem = pl.BlockSpec(memory_space=pltpu.VMEM)
    hbm = pl.BlockSpec(memory_space=pl.ANY)
    density = pl.pallas_call(
        functools.partial(kernel, side, count),
        name="density",
        out_shape=jax.ShapeDtypeStruct((1, points), f32),
        in_specs=[vmem, vmem, hbm, hbm, hbm, hbm],
        out_specs=vmem,
        scratch_shapes=[
            pltpu.VMEM(coeff_rows.shape, bf16),
            pltpu.VMEM(coeff_cols.shape, bf16),
            pltpu.VMEM(row_phi.shape, bf16),
            pltpu.VMEM(col_phi.shape, bf16),
            pltpu.VMEM(coeff_rows.shape, bf16),
            *[pltpu.VMEM((CHUNKS, side, width), f32)] * 2,
            *[pltpu.VMEM((CHUNKS, side, width), bf16)] * 6,
            *[pltpu.VMEM((HEAD + count * side, side), bf16)] * 16,
            dma((3 + CHUNKS,)),
            dma((3, CHUNKS)),
            dma((3, CHUNKS)),
            dma((2, 4, CHUNKS)),
            dma((2, 4, CHUNKS)),
            dma((8, CHUNKS)),
            dma((8, CHUNKS)),
        ],
        compiler_params=pltpu.CompilerParams(
            collective_id=0, has_side_effects=True, vmem_limit_bytes=60 * 1024 * 1024
        ),
    )(occupation.reshape(1, depth), send_list, coeff_rows, coeff_cols, row_phi, col_phi)
    return density.reshape(1, 1, 1, -1)


def solution(mesh):
    in_specs = (
        P("row", "state"),
        P("col", "state"),
        P("state"),
        P("state", "row", "col", None, None),
        P("state", "row", "col", None, None, None),
        P("state", "row", "col", None, None, None),
    )
    out_specs = P("state", "row", "col", None)
    return jax.shard_map(local, mesh=mesh, in_specs=in_specs, out_specs=out_specs, check_vma=False)
```

time: 88.8 us -> 51.2 us (0.58)
  blocking collectives: 80.9 us -> 0 us
  Pallas kernels: 0 us -> 48.4 us
  matrix products: 5.63 us -> 0 us
    pallas_call x0 -> x1, Pallas kernels: none -> 48.4 us  [local(): pl.pallas_call(functools.partial(kernel, side, count), name='density', ou...]
    all_to_all x1 -> x0, blocking collectives: 43.2 us -> none  [local(): lax.all_to_all(outgoing, 'row', split_axis=0, concat_axis=0, tiled=True)]
    psum x1 -> x0, blocking collectives: 37.7 us -> none  [local(): summed = lax.psum(partial_block, 'state')]
    dot_general x3 -> x0, matrix products: 5.63 us -> none  [the longest x1 3.87 us: local(): lax.dot_general(weighted, coeff_cols, (((1,), (1,)), ((), ())), preferred...]
    unnamed x10 -> x2, local copies, waits for them, and re-layouts: 1.68 us -> 2.57 us
where the time goes in v1:
time: 51.2 us; the launch traced here: 51 us
  Pallas kernels  48.4 us (95%)
  local copies, waits for them, and re-layouts  2.57 us (5%)
    pallas_call x1, Pallas kernels, local(): pl.pallas_call(functools.partial(kernel, side, count), name='density', ou...  48.4 us
    unnamed x2, local copies, waits for them, and re-layouts  2.57 us

profile of v1, /device:TPU:1, one launch (start us, length us, event | category | flops | bytes accessed | tf_op | source)
XLA Modules:
  0.0 51.0 jit_solution(17662316465692454510)
XLA Ops:
  0.0 1.3 %copy.7.list_ref = s32[1,1,1,16,2]{4,3,2,1,0:T(8,128)} copy(s32[1,1,1,16,2]{3,4,2,1,0:T(2,128)} %param.9) | data formatting | bytes 256 | tf_op args[3]
  1.3 48.4 %density.1 = f32[1,256]{1,0:T(1,128)} custom-call(f32[1,1024]{1,0:T(1,128)} %bitcast.2, s32[1,1,1,16,2]{4,3,2,1,0:T(8,128)} %copy.7.list_ref, bf16[512,1024]{1,0:T(8,128)(2,1)} %rows_hbm.1, bf16[1024,1024]{1,0:T(8,128)(2,1)} %cols_hbm.1, bf16[1,1,1,32,128,256]{5,4,3,2,1,0:T(8,128)(2,1)} %rphi_hbm.1, bf16[1,1,1,32,128,256]{5,4,3,2,1,0:T(8,128)(2,1)} %cphi_hbm.1), custom_call_target="tpu_custom_call" | custom-call | tf_op jit(solution)/shard_map/density/pallas_call | solution.py:233
  49.8 1.2 %copy.9 = f32[1,1,1,256]{3,2,1,0:T(1,128)} copy(f32[1,1,1,256]{3,2,1,0:T(1,128)} %bitcast.3) | data formatting | bytes 2048

commit v2 on v1

v2 whole, which is shorter than its diff:
```python
import functools

import jax
import jax.numpy as jnp
from jax import lax
from jax.experimental import pallas as pl
from jax.experimental.pallas import tpu as pltpu
from jax.sharding import PartitionSpec as P

MESH = pl.DeviceIdType.MESH
HEAD = 16
FIRST = (0, 1, 2, 4, 6, 7)
TILES = (1, 1, 2, 2, 1, 1)
DOTS = ((0, 1), (2,), (3,), (4, 5))
CHUNKS = len(TILES)
OWN, UP, DOWN, FAR = 0, (0, 1, 2, 3), (0, 4, 5, 6), 7


def kernel(
    side, count, occ_ref, list_ref, rows_hbm, cols_hbm, rphi_hbm, cphi_hbm, out_ref,
    rows_v, cols_v, rphi_v, cphi_v, weighted_v, head_v, *rest,
):
    own_v, next_v, stage_s, stage_r, plain_s, plain_r, comb_s, comb_r = (
        rest[i * CHUNKS : (i + 1) * CHUNKS] for i in range(8)
    )
    rest = rest[8 * CHUNKS :]
    blocks = [[rest[2 * j], rest[2 * j + 1]] for j in range(8)]
    load_sem, xs, xr, ys, yr, ss, sr = rest[16:]
    n_state, n_row = lax.axis_size("state"), lax.axis_size("row")
    chips = n_row // 2
    s, r = lax.axis_index("state"), lax.axis_index("row")
    y, k = r // 2, r % 2
    x_next, x_prev = lax.rem(s + 1, n_state), lax.rem(s + n_state - 1, n_state)
    up = lax.rem(y + 1, chips) * 2 + k
    down = lax.rem(y + chips - 1, chips) * 2 + k
    sibling = y * 2 + 1 - k
    width = count * side // len(DOTS)

    barrier = pltpu.get_barrier_semaphore()
    neighbours = ({"state": x_next}, {"state": x_prev}, {"row": up}, {"row": down}, {"row": sibling})
    for who in neighbours:
        pl.semaphore_signal(barrier, inc=1, device_id=who, device_id_type=MESH)

    def local_copy(src, dst, n):
        copy = pltpu.make_async_copy(src, dst, load_sem.at[n])
        copy.start()
        return copy

    row_loads = []
    for j in range(n_state):
        target = pl.multiple_of(lax.rem(s + j, n_state) * side, side)
        row_loads.append(local_copy(rows_hbm.at[pl.ds(target, side)], rows_v.at[pl.ds(j * side, side)], j))
    col_loads = []
    for g in range(len(DOTS)):
        part = pl.ds(g * width, width)
        col_loads.append(local_copy(cols_hbm.at[part], cols_v.at[part], 4 + g))
    phi_loads = [local_copy(rphi_hbm, rphi_v, 8), local_copy(cphi_hbm, cphi_v, 9)]

    head_v[...] = jnp.zeros_like(head_v)
    head_v[pl.ds(0, 2), pl.ds(0, n_row)] = list_ref[0, 0, 0].astype(jnp.float32)
    blocks[OWN][0][pl.ds(0, HEAD), :] = head_v[...].astype(jnp.bfloat16)

    for j in range(n_state):
        row_loads[j].wait()
        part = rows_v[pl.ds(j * side, side), :].astype(jnp.float32)
        weighted_v[pl.ds(j * side, side), :] = (part * occ_ref[...]).astype(jnp.bfloat16)

    sent = []

    def send(src, dst, send_sem, recv_sem, who):
        copy = pltpu.make_async_remote_copy(
            src_ref=src, dst_ref=dst, send_sem=send_sem, recv_sem=recv_sem, device_id=who, device_id_type=MESH
        )
        copy.start()
        sent.append(copy)

    def arrived(dst, send_sem, recv_sem):
        pltpu.make_async_remote_copy(
            src_ref=dst, dst_ref=dst, send_sem=send_sem, recv_sem=recv_sem,
            device_id={"row": sibling}, device_id_type=MESH,
        ).wait_recv()

    def ways(q):
        return (x_next, x_prev) if q % 2 == 0 else (x_prev, x_next)

    def partials(g):
        col_loads[g].wait()
        product = lax.dot_general(
            weighted_v[...], cols_v[pl.ds(g * width, width), :], (((1,), (1,)), ((), ())),
            preferred_element_type=jnp.float32,
        )
        start = 0
        for q in DOTS[g]:
            part = product[:, start : start + TILES[q] * side]
            start += TILES[q] * side
            after, before = part[side : 2 * side], part[3 * side :]
            relayed, plain = (after, before) if q % 2 == 0 else (before, after)
            stage_s[q][...] = part[2 * side : 3 * side].astype(jnp.bfloat16)
            plain_s[q][...] = plain.astype(jnp.bfloat16)
            next_v[q][...] = relayed
            own_v[q][...] = part[:side]

    def first_sends(q):
        ahead, back = ways(q)
        send(stage_s[q], stage_r[q], xs.at[0, q], xr.at[0, q], {"state": ahead})
        send(plain_s[q], plain_r[q], xs.at[1, q], xr.at[1, q], {"state": back})

    def relay(q):
        ahead, _ = ways(q)
        arrived(stage_r[q], xs.at[0, q], xr.at[0, q])
        comb_s[q][...] = (next_v[q][...] + stage_r[q][...].astype(jnp.float32)).astype(jnp.bfloat16)
        send(comb_s[q], comb_r[q], xs.at[2, q], xr.at[2, q], {"state": ahead})

    def span(q):
        if q == 0:
            return pl.ds(0, HEAD + TILES[0] * side)
        return pl.ds(HEAD + FIRST[q] * side, TILES[q] * side)

    def share(j, q):
        send(blocks[j][0].at[span(q)], blocks[j][1].at[span(q)], ss.at[j, q], sr.at[j, q], {"row": sibling})

    def hop(way, h, q):
        path, who = ((UP, up), (DOWN, down))[way]
        if h == 4 and q % 2 != way:
            return
        src = blocks[path[h - 1]][0].at[span(q)]
        dst = blocks[FAR if h == 4 else path[h]][0].at[span(q)]
        send(src, dst, ys.at[way, h - 1, q], yr.at[way, h - 1, q], {"row": who})

    def finish(q):
        arrived(plain_r[q], xs.at[1, q], xr.at[1, q])
        arrived(comb_r[q], xs.at[2, q], xr.at[2, q])
        total = own_v[q][...] + plain_r[q][...].astype(jnp.float32) + comb_r[q][...].astype(jnp.float32)
        total = total.astype(jnp.bfloat16)
        for t in range(TILES[q]):
            blocks[OWN][0][pl.ds(HEAD + (FIRST[q] + t) * side, side), :] = total[:, t * side : (t + 1) * side]
        hop(0, 1, q)
        hop(1, 1, q)
        share(OWN, q)

    def forward(way, h, q):
        j = FAR if h == 4 else (UP, DOWN)[way][h]
        arrived(blocks[j][0].at[span(q)], ys.at[way, h - 1, q], yr.at[way, h - 1, q])
        if h < 4:
            hop(way, h + 1, q)
        share(j, q)

    def forward_both(h, q):
        forward(0, h, q)
        forward(1, h, q)

    lane_of = lax.broadcasted_iota(jnp.int32, (HEAD, 128), 1)

    def chip_of(j):
        if j == FAR:
            return lax.rem(y + 4, chips)
        if j in UP:
            return lax.rem(y + chips - UP.index(j), chips)
        return lax.rem(y + DOWN.index(j), chips)

    def contract(j, other, total):
        ref = blocks[j][other]
        source = chip_of(j) * 2 + (1 - k if other else k)
        if other:
            for q in range(CHUNKS):
                arrived(ref.at[span(q)], ss.at[j, q], sr.at[j, q])
        head = jnp.where(lane_of == r, ref[pl.ds(0, HEAD), :].astype(jnp.float32), 0.0)
        head = jnp.sum(head, axis=1, keepdims=True)
        wants = [head[slot : slot + 1] for slot in (0, 1)]
        got = [None, None]
        for t in range(count):
            tile = ref[pl.ds(HEAD + t * side, side), :]
            for slot in (0, 1):
                gate = jnp.where(wants[slot] == float(t), 1.0, 0.0)
                gate = jnp.broadcast_to(gate, (side, side)).astype(jnp.bfloat16)
                term = gate * tile
                got[slot] = term if got[slot] is None else got[slot] + term
        for slot in (0, 1):
            m = source * 2 + slot
            half = jnp.dot(got[slot], cphi_v[0, 0, 0, m], preferred_element_type=jnp.float32)
            weighed = rphi_v[0, 0, 0, m].astype(jnp.float32) * half
            total = total + jnp.sum(weighed.reshape(side // 8, 8, weighed.shape[1]), axis=0)
        return total

    partials(0)
    pl.semaphore_wait(barrier, len(neighbours))
    first_sends(0)
    first_sends(1)
    partials(1)
    first_sends(2)
    partials(2)
    partials(3)
    relay(0)
    relay(1)
    first_sends(3)
    relay(2)
    first_sends(4)
    first_sends(5)
    finish(0)
    finish(1)
    relay(3)
    finish(2)
    relay(4)
    relay(5)
    forward_both(1, 0)
    forward_both(1, 1)
    finish(3)
    forward_both(1, 2)
    finish(4)
    finish(5)
    for q in (3, 4, 5):
        forward_both(1, q)
    order = ((0, 2, 4, 1, 3, 5), (1, 3, 5, 0, 2, 4))
    for h in (2, 3):
        for i in range(CHUNKS):
            for way in (0, 1):
                forward(way, h, order[way][i])
    for load in phi_loads:
        load.wait()
    total = jnp.zeros((8, out_ref.shape[-1]), jnp.float32)
    for j in (OWN, UP[1], DOWN[1]):
        for other in (0, 1):
            total = contract(j, other, total)
    forward(0, 4, 0)
    forward(1, 4, 1)
    for j in (UP[2], DOWN[2]):
        for other in (0, 1):
            total = contract(j, other, total)
    for q in (2, 3, 4, 5):
        forward(q % 2, 4, q)
    for j in (UP[3], DOWN[3], FAR):
        for other in (0, 1):
            total = contract(j, other, total)
    out_ref[...] = jnp.sum(total, axis=0, keepdims=True)
    for copy in sent:
        copy.wait_send()


def local(coeff_rows, coeff_cols, occupation, send_list, row_phi, col_phi):
    n_state = lax.axis_size("state")
    rows, depth = coeff_rows.shape
    side = rows // n_state
    count = coeff_cols.shape[0] // side
    points = row_phi.shape[-1]
    bf16, f32 = jnp.bfloat16, jnp.float32
    dma = pltpu.SemaphoreType.DMA
    vmem = pl.BlockSpec(memory_space=pltpu.VMEM)
    hbm = pl.BlockSpec(memory_space=pl.ANY)
    density = pl.pallas_call(
        functools.partial(kernel, side, count),
        name="density",
        out_shape=jax.ShapeDtypeStruct((1, points), f32),
        in_specs=[vmem, vmem, hbm, hbm, hbm, hbm],
        out_specs=vmem,
        scratch_shapes=[
            pltpu.VMEM(coeff_rows.shape, bf16),
            pltpu.VMEM(coeff_cols.shape, bf16),
            pltpu.VMEM(row_phi.shape, bf16),
            pltpu.VMEM(col_phi.shape, bf16),
            pltpu.VMEM(coeff_rows.shape, bf16),
            pltpu.VMEM((HEAD, 128), f32),
            *[pltpu.VMEM((side, n * side), kind) for kind in (f32, f32, *[bf16] * 6) for n in TILES],
            *[pltpu.VMEM((HEAD + count * side, side), bf16)] * 16,
            dma((10,)),
            dma((3, CHUNKS)),
            dma((3, CHUNKS)),
            dma((2, 4, CHUNKS)),
            dma((2, 4, CHUNKS)),
            dma((8, CHUNKS)),
            dma((8, CHUNKS)),
        ],
        compiler_params=pltpu.CompilerParams(
            collective_id=0, has_side_effects=True, vmem_limit_bytes=60 * 1024 * 1024
        ),
    )(occupation.reshape(1, depth), jnp.swapaxes(send_list, 3, 4), coeff_rows, coeff_cols, row_phi, col_phi)
    return density.reshape(1, 1, 1, -1)


def solution(mesh):
    in_specs = (
        P("row", "state"),
        P("col", "state"),
        P("state"),
        P("state", "row", "col", None, None),
        P("state", "row", "col", None, None, None),
        P("state", "row", "col", None, None, None),
    )
    out_specs = P("state", "row", "col", None)
    return jax.shard_map(local, mesh=mesh, in_specs=in_specs, out_specs=out_specs, check_vma=False)
```

time: 51.2 us -> 48.8 us (0.953)
  local copies, waits for them, and re-layouts: 2.57 us -> 1.24 us
  Pallas kernels: 48.4 us -> 47.3 us
    unnamed x2 -> x1, local copies, waits for them, and re-layouts: 2.57 us -> 1.24 us
    pallas_call x1, Pallas kernels: 48.4 us -> 47.3 us  [local(): pl.pallas_call(functools.partial(kernel, side, count), name='density', ou...]
where the time goes in v2:
time: 48.8 us; the launch traced here: 48.6 us
  Pallas kernels  47.3 us (97%)
  local copies, waits for them, and re-layouts  1.24 us (3%)
    pallas_call x1, Pallas kernels, local(): pl.pallas_call(functools.partial(kernel, side, count), name='density', ou...  47.3 us
    unnamed x1, local copies, waits for them, and re-layouts  1.24 us

profile of v2, /device:TPU:1, one launch (start us, length us, event | category | flops | bytes accessed | tf_op | source)
XLA Modules:
  0.0 48.6 jit_solution(6616172414220896393)
XLA Ops:
  0.0 47.3 %density.1 = f32[1,256]{1,0:T(1,128)} custom-call(f32[1,1024]{1,0:T(1,128)} %bitcast.3, s32[1,1,1,2,16]{4,3,2,1,0:T(2,128)} %bitcast.5, bf16[512,1024]{1,0:T(8,128)(2,1)} %rows_hbm.1, bf16[1024,1024]{1,0:T(8,128)(2,1)} %cols_hbm.1, bf16[1,1,1,32,128,256]{5,4,3,2,1,0:T(8,128)(2,1)} %rphi_hbm.1, bf16[1,1,1,32,128,256]{5,4,3,2,1,0:T(8,128)(2,1)} %cphi_hbm.1), custom_call_target="tpu_custom_call" | custom-call | tf_op jit(solution)/shard_map/density/pallas_call | solution.py:249
  47.3 1.2 %copy.8 = f32[1,1,1,256]{3,2,1,0:T(1,128)} copy(f32[1,1,1,256]{3,2,1,0:T(1,128)} %bitcast.4) | data formatting | bytes 2048

commit v3 on v2

--- a/solution.py
+++ b/solution.py
@@ -12,20 +12,35 @@
 FIRST = (0, 1, 2, 4, 6, 7)
 TILES = (1, 1, 2, 2, 1, 1)
 DOTS = ((0, 1), (2,), (3,), (4, 5))
+STEPS = (
+    ("dot", 0), ("first", 0), ("first", 1), ("dot", 1), ("first", 2), ("dot", 2), ("dot", 3), ("relay", 0),
+    ("relay", 1), ("first", 3), ("relay", 2), ("first", 4), ("first", 5), ("fin", 0), ("fin", 1), ("relay", 3),
+    ("fin", 2), ("relay", 4), ("relay", 5), ("fwd", 0, 1, 0), ("fwd", 1, 1, 0), ("fwd", 0, 1, 1), ("fwd", 1, 1, 1),
+    ("fin", 3), ("fwd", 0, 1, 2), ("fwd", 1, 1, 2), ("fin", 4), ("fin", 5), ("fwd", 0, 1, 3), ("fwd", 1, 1, 3),
+    ("fwd", 0, 1, 4), ("fwd", 1, 1, 4), ("fwd", 0, 1, 5), ("fwd", 1, 1, 5), ("fwd", 0, 2, 0), ("fwd", 1, 2, 1),
+    ("fwd", 0, 2, 2), ("fwd", 1, 2, 3), ("fwd", 0, 2, 4), ("fwd", 1, 2, 5), ("fwd", 0, 2, 1), ("fwd", 1, 2, 0),
+    ("fwd", 0, 2, 3), ("fwd", 1, 2, 2), ("fwd", 0, 2, 5), ("fwd", 1, 2, 4), ("give", 0), ("give", 1), ("give", 4),
+    ("fwd", 0, 3, 0), ("fwd", 1, 3, 1), ("fwd", 0, 3, 2), ("fwd", 1, 3, 3), ("fwd", 0, 3, 4), ("fwd", 1, 3, 5),
+    ("fwd", 0, 3, 1), ("fwd", 1, 3, 0), ("fwd", 0, 3, 3), ("fwd", 1, 3, 2), ("fwd", 0, 3, 5), ("fwd", 1, 3, 4),
+    ("give", 2), ("give", 5), ("give", 3), ("give", 6), ("keep", 0), ("keep", 1), ("keep", 4), ("take", 0),
+    ("take", 1), ("take", 4), ("keep", 2), ("keep", 5), ("fwd", 0, 4, 0), ("fwd", 1, 4, 1), ("fwd", 0, 4, 2),
+    ("fwd", 1, 4, 3), ("fwd", 0, 4, 4), ("fwd", 1, 4, 5), ("give", 7), ("keep", 3), ("keep", 6), ("keep", 7),
+    ("take", 2), ("take", 5), ("take", 3), ("take", 6), ("take", 7),
+)
 CHUNKS = len(TILES)
 OWN, UP, DOWN, FAR = 0, (0, 1, 2, 3), (0, 4, 5, 6), 7
 
 
 def kernel(
-    side, count, occ_ref, list_ref, rows_hbm, cols_hbm, rphi_hbm, cphi_hbm, out_ref,
-    rows_v, cols_v, rphi_v, cphi_v, weighted_v, head_v, *rest,
+    side, count, occ_hbm, list_hbm, rows_hbm, cols_hbm, rphi_hbm, cphi_hbm, out_ref,
+    rows_v, cols_v, rphi_v, cphi_v, weighted_v, head_v, occ_ref, list_ref, *rest,
 ):
     own_v, next_v, stage_s, stage_r, plain_s, plain_r, comb_s, comb_r = (
         rest[i * CHUNKS : (i + 1) * CHUNKS] for i in range(8)
     )
     rest = rest[8 * CHUNKS :]
-    blocks = [[rest[2 * j], rest[2 * j + 1]] for j in range(8)]
-    load_sem, xs, xr, ys, yr, ss, sr = rest[16:]
+    blocks = rest[:8]
+    give_s, give_r, load_sem, xs, xr, ys, yr, gs, gr = rest[8:]
     n_state, n_row = lax.axis_size("state"), lax.axis_size("row")
     chips = n_row // 2
     s, r = lax.axis_index("state"), lax.axis_index("row")
@@ -46,6 +61,8 @@
         copy.start()
         return copy
 
+    occ_load = local_copy(occ_hbm, occ_ref, 10)
+    list_load = local_copy(list_hbm, list_ref, 11)
     row_loads = []
     for j in range(n_state):
         target = pl.multiple_of(lax.rem(s + j, n_state) * side, side)
@@ -54,12 +71,8 @@
     for g in range(len(DOTS)):
         part = pl.ds(g * width, width)
         col_loads.append(local_copy(cols_hbm.at[part], cols_v.at[part], 4 + g))
-    phi_loads = [local_copy(rphi_hbm, rphi_v, 8), local_copy(cphi_hbm, cphi_v, 9)]
-
-    head_v[...] = jnp.zeros_like(head_v)
-    head_v[pl.ds(0, 2), pl.ds(0, n_row)] = list_ref[0, 0, 0].astype(jnp.float32)
-    blocks[OWN][0][pl.ds(0, HEAD), :] = head_v[...].astype(jnp.bfloat16)
-
+
+    occ_load.wait()
     for j in range(n_state):
         row_loads[j].wait()
         part = rows_v[pl.ds(j * side, side), :].astype(jnp.float32)
@@ -116,38 +129,30 @@
             return pl.ds(0, HEAD + TILES[0] * side)
         return pl.ds(HEAD + FIRST[q] * side, TILES[q] * side)
 
-    def share(j, q):
-        send(blocks[j][0].at[span(q)], blocks[j][1].at[span(q)], ss.at[j, q], sr.at[j, q], {"row": sibling})
-
     def hop(way, h, q):
         path, who = ((UP, up), (DOWN, down))[way]
         if h == 4 and q % 2 != way:
             return
-        src = blocks[path[h - 1]][0].at[span(q)]
-        dst = blocks[FAR if h == 4 else path[h]][0].at[span(q)]
+        src = blocks[path[h - 1]].at[span(q)]
+        dst = blocks[FAR if h == 4 else path[h]].at[span(q)]
         send(src, dst, ys.at[way, h - 1, q], yr.at[way, h - 1, q], {"row": who})
 
     def finish(q):
         arrived(plain_r[q], xs.at[1, q], xr.at[1, q])
         arrived(comb_r[q], xs.at[2, q], xr.at[2, q])
-        total = own_v[q][...] + plain_r[q][...].astype(jnp.float32) + comb_r[q][...].astype(jnp.float32)
+        total = own_v[q][...]
+        total = total + plain_r[q][...].astype(jnp.float32) + comb_r[q][...].astype(jnp.float32)
         total = total.astype(jnp.bfloat16)
         for t in range(TILES[q]):
-            blocks[OWN][0][pl.ds(HEAD + (FIRST[q] + t) * side, side), :] = total[:, t * side : (t + 1) * side]
+            blocks[OWN][pl.ds(HEAD + (FIRST[q] + t) * side, side), :] = total[:, t * side : (t + 1) * side]
         hop(0, 1, q)
         hop(1, 1, q)
-        share(OWN, q)
 
     def forward(way, h, q):
         j = FAR if h == 4 else (UP, DOWN)[way][h]
-        arrived(blocks[j][0].at[span(q)], ys.at[way, h - 1, q], yr.at[way, h - 1, q])
+        arrived(blocks[j].at[span(q)], ys.at[way, h - 1, q], yr.at[way, h - 1, q])
         if h < 4:
             hop(way, h + 1, q)
-        share(j, q)
-
-    def forward_both(h, q):
-        forward(0, h, q)
-        forward(1, h, q)
 
     lane_of = lax.broadcasted_iota(jnp.int32, (HEAD, 128), 1)
 
@@ -158,80 +163,60 @@
             return lax.rem(y + chips - UP.index(j), chips)
         return lax.rem(y + DOWN.index(j), chips)
 
-    def contract(j, other, total):
-        ref = blocks[j][other]
-        source = chip_of(j) * 2 + (1 - k if other else k)
-        if other:
-            for q in range(CHUNKS):
-                arrived(ref.at[span(q)], ss.at[j, q], sr.at[j, q])
-        head = jnp.where(lane_of == r, ref[pl.ds(0, HEAD), :].astype(jnp.float32), 0.0)
+    def picked(j, owner):
+        ref = blocks[j]
+        head = jnp.where(lane_of == owner, ref[pl.ds(0, HEAD), :].astype(jnp.float32), 0.0)
         head = jnp.sum(head, axis=1, keepdims=True)
-        wants = [head[slot : slot + 1] for slot in (0, 1)]
         got = [None, None]
         for t in range(count):
             tile = ref[pl.ds(HEAD + t * side, side), :]
             for slot in (0, 1):
-                gate = jnp.where(wants[slot] == float(t), 1.0, 0.0)
+                gate = jnp.where(head[slot : slot + 1] == float(t), 1.0, 0.0)
                 gate = jnp.broadcast_to(gate, (side, side)).astype(jnp.bfloat16)
                 term = gate * tile
                 got[slot] = term if got[slot] is None else got[slot] + term
+        return got
+
+    def contract(source, got):
+        while phi_loads:
+            phi_loads.pop().wait()
         for slot in (0, 1):
             m = source * 2 + slot
             half = jnp.dot(got[slot], cphi_v[0, 0, 0, m], preferred_element_type=jnp.float32)
             weighed = rphi_v[0, 0, 0, m].astype(jnp.float32) * half
-            total = total + jnp.sum(weighed.reshape(side // 8, 8, weighed.shape[1]), axis=0)
-        return total
-
-    partials(0)
-    pl.semaphore_wait(barrier, len(neighbours))
-    first_sends(0)
-    first_sends(1)
-    partials(1)
-    first_sends(2)
-    partials(2)
-    partials(3)
-    relay(0)
-    relay(1)
-    first_sends(3)
-    relay(2)
-    first_sends(4)
-    first_sends(5)
-    finish(0)
-    finish(1)
-    relay(3)
-    finish(2)
-    relay(4)
-    relay(5)
-    forward_both(1, 0)
-    forward_both(1, 1)
-    finish(3)
-    forward_both(1, 2)
-    finish(4)
-    finish(5)
-    for q in (3, 4, 5):
-        forward_both(1, q)
-    order = ((0, 2, 4, 1, 3, 5), (1, 3, 5, 0, 2, 4))
-    for h in (2, 3):
-        for i in range(CHUNKS):
-            for way in (0, 1):
-                forward(way, h, order[way][i])
-    for load in phi_loads:
-        load.wait()
-    total = jnp.zeros((8, out_ref.shape[-1]), jnp.float32)
-    for j in (OWN, UP[1], DOWN[1]):
-        for other in (0, 1):
-            total = contract(j, other, total)
-    forward(0, 4, 0)
-    forward(1, 4, 1)
-    for j in (UP[2], DOWN[2]):
-        for other in (0, 1):
-            total = contract(j, other, total)
-    for q in (2, 3, 4, 5):
-        forward(q % 2, 4, q)
-    for j in (UP[3], DOWN[3], FAR):
-        for other in (0, 1):
-            total = contract(j, other, total)
-    out_ref[...] = jnp.sum(total, axis=0, keepdims=True)
+            part = jnp.sum(weighed.reshape(side // 8, 8, weighed.shape[1]), axis=0)
+            totals[:] = [totals[0] + part] if totals else [part]
+
+    def give(j):
+        for slot, tile in enumerate(picked(j, sibling)):
+            give_s[j, slot] = tile
+        send(give_s.at[j], give_r.at[j], gs.at[j], gr.at[j], {"row": sibling})
+
+    def keep(j):
+        contract(chip_of(j) * 2 + k, picked(j, r))
+
+    def take(j):
+        arrived(give_r.at[j], gs.at[j], gr.at[j])
+        contract(chip_of(j) * 2 + 1 - k, [give_r[j, slot] for slot in (0, 1)])
+
+    def dot(g):
+        partials(g)
+        if g == 0:
+            pl.semaphore_wait(barrier, len(neighbours))
+            list_load.wait()
+            head_v[...] = jnp.zeros_like(head_v)
+            head_v[pl.ds(0, 2), pl.ds(0, n_row)] = list_ref[0, 0, 0].astype(jnp.float32)
+            blocks[OWN][pl.ds(0, HEAD), :] = head_v[...].astype(jnp.bfloat16)
+        if g == len(DOTS) - 1:
+            phi_loads.append(local_copy(rphi_hbm, rphi_v, 8))
+            phi_loads.append(local_copy(cphi_hbm, cphi_v, 9))
+
+    phi_loads, totals = [], []
+    act = {"dot": dot, "first": first_sends, "relay": relay, "fin": finish, "fwd": forward}
+    act |= {"give": give, "keep": keep, "take": take}
+    for step in STEPS:
+        act[step[0]](*step[1:])
+    out_ref[...] = jnp.sum(totals[0], axis=0, keepdims=True)
     for copy in sent:
         copy.wait_send()
 
@@ -250,7 +235,7 @@
         functools.partial(kernel, side, count),
         name="density",
         out_shape=jax.ShapeDtypeStruct((1, points), f32),
-        in_specs=[vmem, vmem, hbm, hbm, hbm, hbm],
+        in_specs=[hbm] * 6,
         out_specs=vmem,
         scratch_shapes=[
             pltpu.VMEM(coeff_rows.shape, bf16),
@@ -259,15 +244,18 @@
             pltpu.VMEM(col_phi.shape, bf16),
             pltpu.VMEM(coeff_rows.shape, bf16),
             pltpu.VMEM((HEAD, 128), f32),
+            pltpu.VMEM((1, depth), f32),
+            pltpu.VMEM((1, 1, 1) + send_list.shape[:2:-1], jnp.int32),
             *[pltpu.VMEM((side, n * side), kind) for kind in (f32, f32, *[bf16] * 6) for n in TILES],
-            *[pltpu.VMEM((HEAD + count * side, side), bf16)] * 16,
-            dma((10,)),
+            *[pltpu.VMEM((HEAD + count * side, side), bf16)] * 8,
+            *[pltpu.VMEM((8, 2, side, side), bf16)] * 2,
+            dma((12,)),
             dma((3, CHUNKS)),
             dma((3, CHUNKS)),
             dma((2, 4, CHUNKS)),
             dma((2, 4, CHUNKS)),
-            dma((8, CHUNKS)),
-            dma((8, CHUNKS)),
+            dma((8,)),
+            dma((8,)),
         ],
         compiler_params=pltpu.CompilerParams(
             collective_id=0, has_side_effects=True, vmem_limit_bytes=60 * 1024 * 1024

time: 48.8 us -> 46.9 us (0.961)
  Pallas kernels: 47.3 us -> 45.5 us
    pallas_call x1, Pallas kernels: 47.3 us -> 45.5 us  [local(): pl.pallas_call(functools.partial(kernel, side, count), name='density', ou...]
where the time goes in v3:
time: 46.9 us; the launch traced here: 46.7 us
  Pallas kernels  45.5 us (97%)
  local copies, waits for them, and re-layouts  1.24 us (3%)
    pallas_call x1, Pallas kernels, local(): pl.pallas_call(functools.partial(kernel, side, count), name='density', ou...  45.5 us
    unnamed x1, local copies, waits for them, and re-layouts  1.24 us

profile of v3, /device:TPU:1, one launch (start us, length us, event | category | flops | bytes accessed | tf_op | source)
XLA Modules:
  0.0 46.7 jit_solution(1607966739736403897)
XLA Ops:
  0.0 45.5 %density.1 = f32[1,256]{1,0:T(1,128)} custom-call(f32[1,1024]{1,0:T(1,128)} %bitcast.3, s32[1,1,1,2,16]{4,3,2,1,0:T(2,128)} %bitcast.5, bf16[512,1024]{1,0:T(8,128)(2,1)} %rows_hbm.1, bf16[1024,1024]{1,0:T(8,128)(2,1)} %cols_hbm.1, bf16[1,1,1,32,128,256]{5,4,3,2,1,0:T(8,128)(2,1)} %rphi_hbm.1, bf16[1,1,1,32,128,256]{5,4,3,2,1,0:T(8,128)(2,1)} %cphi_hbm.1), custom_call_target="tpu_custom_call" | custom-call | tf_op jit(solution)/shard_map/density/pallas_call | solution.py:234
  45.5 1.2 %copy.8 = f32[1,1,1,256]{3,2,1,0:T(1,128)} copy(f32[1,1,1,256]{3,2,1,0:T(1,128)} %bitcast.4) | data formatting | bytes 2048

commit v4 on v3

--- a/solution.py
+++ b/solution.py
@@ -19,13 +19,13 @@
     ("fin", 3), ("fwd", 0, 1, 2), ("fwd", 1, 1, 2), ("fin", 4), ("fin", 5), ("fwd", 0, 1, 3), ("fwd", 1, 1, 3),
     ("fwd", 0, 1, 4), ("fwd", 1, 1, 4), ("fwd", 0, 1, 5), ("fwd", 1, 1, 5), ("fwd", 0, 2, 0), ("fwd", 1, 2, 1),
     ("fwd", 0, 2, 2), ("fwd", 1, 2, 3), ("fwd", 0, 2, 4), ("fwd", 1, 2, 5), ("fwd", 0, 2, 1), ("fwd", 1, 2, 0),
-    ("fwd", 0, 2, 3), ("fwd", 1, 2, 2), ("fwd", 0, 2, 5), ("fwd", 1, 2, 4), ("give", 0), ("give", 1), ("give", 4),
-    ("fwd", 0, 3, 0), ("fwd", 1, 3, 1), ("fwd", 0, 3, 2), ("fwd", 1, 3, 3), ("fwd", 0, 3, 4), ("fwd", 1, 3, 5),
-    ("fwd", 0, 3, 1), ("fwd", 1, 3, 0), ("fwd", 0, 3, 3), ("fwd", 1, 3, 2), ("fwd", 0, 3, 5), ("fwd", 1, 3, 4),
-    ("give", 2), ("give", 5), ("give", 3), ("give", 6), ("keep", 0), ("keep", 1), ("keep", 4), ("take", 0),
-    ("take", 1), ("take", 4), ("keep", 2), ("keep", 5), ("fwd", 0, 4, 0), ("fwd", 1, 4, 1), ("fwd", 0, 4, 2),
-    ("fwd", 1, 4, 3), ("fwd", 0, 4, 4), ("fwd", 1, 4, 5), ("give", 7), ("keep", 3), ("keep", 6), ("keep", 7),
-    ("take", 2), ("take", 5), ("take", 3), ("take", 6), ("take", 7),
+    ("fwd", 0, 2, 3), ("fwd", 1, 2, 2), ("fwd", 0, 2, 5), ("fwd", 1, 2, 4), ("fwd", 0, 3, 0), ("fwd", 1, 3, 1),
+    ("fwd", 0, 3, 2), ("fwd", 1, 3, 3), ("give", 0), ("give", 1), ("give", 4), ("keep", 0), ("fwd", 0, 3, 4),
+    ("fwd", 1, 3, 5), ("fwd", 0, 3, 1), ("fwd", 1, 3, 0), ("keep", 1), ("keep", 4), ("fwd", 0, 3, 3),
+    ("fwd", 1, 3, 2), ("fwd", 0, 3, 5), ("fwd", 1, 3, 4), ("give", 2), ("give", 5), ("give", 3), ("give", 6),
+    ("take", 0), ("take", 1), ("take", 4), ("keep", 2), ("keep", 5), ("keep", 3), ("keep", 6), ("take", 2),
+    ("take", 5), ("drain", 20), ("fwd", 0, 4, 0), ("fwd", 1, 4, 1), ("fwd", 0, 4, 2), ("fwd", 1, 4, 3),
+    ("fwd", 0, 4, 4), ("fwd", 1, 4, 5), ("give", 7), ("keep", 7), ("take", 3), ("take", 6), ("take", 7),
 )
 CHUNKS = len(TILES)
 OWN, UP, DOWN, FAR = 0, (0, 1, 2, 3), (0, 4, 5, 6), 7
@@ -199,6 +199,10 @@
         arrived(give_r.at[j], gs.at[j], gr.at[j])
         contract(chip_of(j) * 2 + 1 - k, [give_r[j, slot] for slot in (0, 1)])
 
+    def drain(left):
+        while len(sent) > left:
+            sent.pop(0).wait_send()
+
     def dot(g):
         partials(g)
         if g == 0:
@@ -213,12 +217,11 @@
 
     phi_loads, totals = [], []
     act = {"dot": dot, "first": first_sends, "relay": relay, "fin": finish, "fwd": forward}
-    act |= {"give": give, "keep": keep, "take": take}
+    act |= {"give": give, "keep": keep, "take": take, "drain": drain}
     for step in STEPS:
         act[step[0]](*step[1:])
     out_ref[...] = jnp.sum(totals[0], axis=0, keepdims=True)
-    for copy in sent:
-        copy.wait_send()
+    drain(0)
 
 
 def local(coeff_rows, coeff_cols, occupation, send_list, row_phi, col_phi):

time: 46.9 us -> 46.9 us (level)
  no operation moved by 1% of the time
where the time goes in v4:
time: 46.9 us; the launch traced here: 46.8 us
  Pallas kernels  45.5 us (97%)
  local copies, waits for them, and re-layouts  1.24 us (3%)
    pallas_call x1, Pallas kernels, local(): pl.pallas_call(functools.partial(kernel, side, count), name='density', ou...  45.5 us
    unnamed x1, local copies, waits for them, and re-layouts  1.24 us

profile of v4, /device:TPU:1, one launch (start us, length us, event | category | flops | bytes accessed | tf_op | source)
XLA Modules:
  0.0 46.8 jit_solution(2958009366015288157)
XLA Ops:
  0.0 45.5 %density.1 = f32[1,256]{1,0:T(1,128)} custom-call(f32[1,1024]{1,0:T(1,128)} %bitcast.3, s32[1,1,1,2,16]{4,3,2,1,0:T(2,128)} %bitcast.5, bf16[512,1024]{1,0:T(8,128)(2,1)} %rows_hbm.1, bf16[1024,1024]{1,0:T(8,128)(2,1)} %cols_hbm.1, bf16[1,1,1,32,128,256]{5,4,3,2,1,0:T(8,128)(2,1)} %rphi_hbm.1, bf16[1,1,1,32,128,256]{5,4,3,2,1,0:T(8,128)(2,1)} %cphi_hbm.1), custom_call_target="tpu_custom_call" | custom-call | tf_op jit(solution)/shard_map/density/pallas_call | solution.py:237
  45.5 1.2 %copy.8 = f32[1,1,1,256]{3,2,1,0:T(1,128)} copy(f32[1,1,1,256]{3,2,1,0:T(1,128)} %bitcast.4) | data formatting | bytes 2048
